TPU v7x, 128 devices: a whole 4x4x4 slice. The times are simulated.
128 devices in a mesh: phi: 16 (over y_hi, z, core), gz: 8 (over y_lo, x).
Axes of the slice: x: 4, y: 4 (y_hi: 2, y_lo: 2; y = y_hi * 2 + y_lo), z: 4, core: 2. Of those that a mesh axis runs over, the one named last changes fastest.
Arguments:
- electric_radial: float32 [192, 128, 2048], P('gz', None, 'phi'), may hold values from -6 to 6
- electric_azimuth: float32 [192, 128, 2048], P('gz', None, 'phi'), may hold values from -6 to 6
- electric_height: float32 [192, 128, 2048], P('gz', None, 'phi'), may hold values from -6 to 6
- magnetic_radial: float32 [192, 128, 2048], P('gz', None, 'phi'), may hold values from -6 to 6
- magnetic_azimuth: float32 [192, 128, 2048], P('gz', None, 'phi'), may hold values from -6 to 6
- magnetic_height: float32 [192, 128, 2048], P('gz', None, 'phi'), may hold values from -6 to 6
- material: int32 [192, 128, 2048], P('gz', None, 'phi'), may hold values from 0 to 7
- permittivity: float32 [8], replicated, may hold values from 1 to 10
- conductivity: float32 [8], replicated, may hold values from 0.05 to 5
- mode_cutoff: int32 [32], replicated, may hold values from 1 to 127, as said below
Outputs:
- updated_electric_radial: float32 [192, 128, 2048], P('gz', None, 'phi')
- updated_electric_azimuth: float32 [192, 128, 2048], P('gz', None, 'phi')
- updated_electric_height: float32 [192, 128, 2048], P('gz', None, 'phi')
- updated_magnetic_radial: float32 [192, 128, 2048], P('gz', None, 'phi')
- updated_magnetic_azimuth: float32 [192, 128, 2048], P('gz', None, 'phi')
- updated_magnetic_height: float32 [192, 128, 2048], P('gz', None, 'phi')
Inputs may be any that keep to these rules, and one draw needn't show every extreme that they name: `mode_cutoff`: cutoffs never fall from one filtered row to the next outward, and the outermost filtered row's cutoff is 127.
All inputs are finite; a program needn't handle non-finite values.
Results may differ from a plain program's by a relative error of at most 0.00005.
Values sent between devices are 32-bit elements; how exact they have to be, the bound alone decides.
A program may use at most 128 MiB of HBM per device.

v0:
```python
import math
import jax
import jax.numpy as jnp
from jax import lax
from jax.sharding import PartitionSpec as P

KMAX = 128
NF = 32
NMAT = 8
inner_radius = 64.0
time_step = 0.2


def shifted(block, axis, distance):
    devices = range(lax.axis_size(axis))
    route = [((i - distance) % len(devices), i) for i in devices]
    return lax.ppermute(block, axis, route)


def shifted_2(block, axis, distance):
    devices = range(lax.axis_size(axis))
    route = [(i - distance, i) for i in devices if i - distance in devices]
    return lax.ppermute(block, axis, route)


def radial_forward(values):
    zero_slab = jnp.zeros_like(values[:, :1, :])
    return jnp.concatenate([values[:, 1:, :], zero_slab], axis=1) - values


def radial_backward(values):
    zero_slab = jnp.zeros_like(values[:, :1, :])
    return values - jnp.concatenate([zero_slab, values[:, :-1, :]], axis=1)


def ahead_azimuth(values, border):
    return jnp.concatenate([values[:, :, 1:], border[:, :, None]], axis=2) - values


def behind_azimuth(values, border):
    return values - jnp.concatenate([border[:, :, None], values[:, :, :-1]], axis=2)


def ahead_height(values, border):
    return jnp.concatenate([values[1:], border[None]], axis=0) - values


def behind_height(values, border):
    return values - jnp.concatenate([border[None], values[:-1]], axis=0)


def cycle_basis(offset, length, cycle_size):
    columns = offset + jnp.arange(length, dtype=jnp.int32)
    mode_index = jnp.arange(KMAX, dtype=jnp.int32)
    angles = (columns[:, None] * mode_index[None, :] % cycle_size).astype(jnp.float32) * (
        2.0 * math.pi / cycle_size
    )
    return jnp.concatenate([jnp.cos(angles), jnp.sin(angles)], axis=1)


def mode_weights(cutoffs, cycle_size):
    mode_index = jnp.arange(KMAX, dtype=jnp.int32)
    scaled = jnp.where(mode_index == 0, 1.0, 2.0).astype(jnp.float32) / cycle_size
    weights = jnp.where(mode_index[None, :] <= cutoffs[:, None], scaled[None, :], 0.0)
    return jnp.concatenate([weights, weights], axis=1)


def transform(block, basis):
    flat = block.reshape(-1, block.shape[-1])
    result = jnp.dot(
        flat, basis, precision=lax.Precision.HIGHEST, preferred_element_type=jnp.float32
    )
    return result.reshape(block.shape[:-1] + (basis.shape[1],))


def synthesize(spectrum, basis):
    flat = spectrum.reshape(-1, spectrum.shape[-1])
    result = jnp.dot(
        flat, basis.T, precision=lax.Precision.HIGHEST, preferred_element_type=jnp.float32
    )
    return result.reshape(spectrum.shape[:-1] + (basis.shape[0],))


def cycle_filter(stacked, mode_cutoff):
    cycle_count = lax.axis_size("phi")
    local_width = stacked.shape[3]
    cycle_size = cycle_count * local_width
    offset = lax.axis_index("phi") * local_width
    weights = mode_weights(mode_cutoff, cycle_size)
    local_basis = cycle_basis(offset, local_width, cycle_size)
    portion = lax.all_gather(stacked, "phi", axis=3, tiled=True)
    spectrum = transform(portion, cycle_basis(jnp.int32(0), portion.shape[3], cycle_size))
    return synthesize(spectrum * weights[None, None], local_basis)


def filter_three(first, second, third, mode_cutoff):
    stacked = jnp.stack([first[:, :NF], second[:, :NF], third[:, :NF]])
    filtered = cycle_filter(stacked, mode_cutoff)
    return (
        jnp.concatenate([filtered[0], first[:, NF:]], axis=1),
        jnp.concatenate([filtered[1], second[:, NF:]], axis=1),
        jnp.concatenate([filtered[2], third[:, NF:]], axis=1),
    )


def local(
    electric_radial,
    electric_azimuth,
    electric_height,
    magnetic_radial,
    magnetic_azimuth,
    magnetic_height,
    material,
    permittivity,
    conductivity,
    mode_cutoff,
):
    local_width = electric_radial.shape[2]
    radial_rows = electric_radial.shape[1]
    node_radius = (inner_radius + jnp.arange(radial_rows, dtype=jnp.float32))[None, :, None]
    center_radius = node_radius + 0.5
    angle_step = 2.0 * math.pi / (lax.axis_size("phi") * local_width)
    border_height, border_radial = shifted(
        (electric_height[:, :, 0], electric_radial[:, :, 0]), "phi", -1
    )
    upper_azimuth, upper_radial = shifted_2((electric_azimuth[0], electric_radial[0]), "gz", -1)
    radial_half = magnetic_radial - time_step * (
        ahead_azimuth(electric_height, border_height) / (node_radius * angle_step)
        - ahead_height(electric_azimuth, upper_azimuth)
    )
    azimuth_half = magnetic_azimuth - time_step * (
        ahead_height(electric_radial, upper_radial) - radial_forward(electric_height)
    )
    height_half = magnetic_height - time_step * (
        radial_forward(node_radius * electric_azimuth) / center_radius
        - ahead_azimuth(electric_radial, border_radial) / (center_radius * angle_step)
    )
    new_hr, new_hp, new_hz = filter_three(radial_half, azimuth_half, height_half, mode_cutoff)
    epsilon = jnp.zeros(material.shape, jnp.float32)
    sigma_cell = jnp.zeros(material.shape, jnp.float32)
    for number in range(NMAT):
        epsilon = jnp.where(material == number, permittivity[number], epsilon)
        sigma_cell = jnp.where(material == number, conductivity[number], sigma_cell)
    losses = sigma_cell * time_step / (2.0 * epsilon)
    keep_factor = (1.0 - losses) / (1.0 + losses)
    drive_factor = time_step / (epsilon * (1.0 + losses))
    before_height, before_radial = shifted((new_hz[:, :, -1], new_hr[:, :, -1]), "phi", 1)
    lower_azimuth, lower_radial = shifted_2((new_hp[-1], new_hr[-1]), "gz", 1)
    radial_next = keep_factor * electric_radial + drive_factor * (
        behind_azimuth(new_hz, before_height) / (center_radius * angle_step)
        - behind_height(new_hp, lower_azimuth)
    )
    azimuth_next = keep_factor * electric_azimuth + drive_factor * (
        behind_height(new_hr, lower_radial) - radial_backward(new_hp)
    )
    height_next = keep_factor * electric_height + drive_factor * (
        radial_backward(center_radius * new_hp) / node_radius
        - behind_azimuth(new_hr, before_radial) / (node_radius * angle_step)
    )
    new_er, new_ep, new_ez = filter_three(radial_next, azimuth_next, height_next, mode_cutoff)
    return (new_er, new_ep, new_ez, new_hr, new_hp, new_hz)


def solution(mesh):
    placed = (
        P("gz", None, "phi"),
        P("gz", None, "phi"),
        P("gz", None, "phi"),
        P("gz", None, "phi"),
        P("gz", None, "phi"),
        P("gz", None, "phi"),
        P("gz", None, "phi"),
        P(),
        P(),
        P(),
    )
    return jax.shard_map(
        local,
        mesh=mesh,
        in_specs=placed,
        out_specs=(
            P("gz", None, "phi"),
            P("gz", None, "phi"),
            P("gz", None, "phi"),
            P("gz", None, "phi"),
            P("gz", None, "phi"),
            P("gz", None, "phi"),
        ),
        check_vma=False,
    )
```

profile of v0, /device:TPU:1, one launch (start us, length us, event | category | flops | bytes accessed | tf_op | source)
XLA Modules:
  0.0 429.9 jit_solution(6858078280458074750)
XLA Ops:
  7.2 2.0 copy.33
  9.3 1.5 collective-permute-start
  11.2 6.2 %collective-permute-start.3 = (f32[24,128]{1,0:T(8,128)S(1)}, f32[24,128]{1,0:T(8,128)S(1)}, u32[]{:S(2)}, u32[]{:S(2)}) collective-permute-start(f32[24,128]{1,0:T(8,128)S(1)} %bitcast.96), channel_id=1, source_target_pairs={{8,0},{16,8},{24,16},{32,24},{40,32},{48,40},{56,48},{64,56},{72,6... | collective-permute-start | bytes 36872 | tf_op jit(solution)/shard_map/ppermute | solution.py:17
  17.4 1.3 collective-permute-start.2
  18.7 1.3 collective-permute-start.1
  20.1 1.2 slice.186
  21.3 1.3 slice.189
  23.3 1.6 slice.184
  24.9 1.3 slice.191
  26.2 1.6 slice.194
  27.8 1.7 copy.29
  29.5 1.7 copy.27
  31.2 5.6 %fusion.14 = (f32[24,128,128]{2,1,0:T(8,128)S(1)}, f32[24,128,128]{2,1,0:T(8,128)S(1)}, f32[24,128,128]{2,1,0:T(8,128)S(1)}) fusion(f32[24,128,128]{2,1,0:T(8,128)} %param.13, f32[24,128,128]{2,1,0:T(8,128)S(1)} %copy-done.1, f32[24,128,1]{2,1,0:T(8,128)} %copy.27, f32[24,128,127]{2,1,0:T(8,128)} %slice.184, f32[24,128,128]{2,1,0:T(8,128)} %param.11, ...), kind=kLoop, calls=%fused_computation.37 | loop fusion | flops 5898240 | bytes 18863104 | tf_op jit(solution)/shard_map/sub | solution.py:127
  37.0 2.3 copy-done.20
  39.8 1.0 fusion.21
  40.9 1.0 copy-done.16
  41.9 1.1 pad_maximum_fusion.6
  45.1 5.0 %fusion.41 = (f32[2048,128]{1,0:T(8,128)}, f32[2048,128]{1,0:T(8,128)}) fusion(), kind=kLoop, calls=%fused_computation.93 | loop fusion | flops 3670016 | bytes 2097152 | tf_op jit(solution)/shard_map/sin | solution.py:58
  50.1 1.5 slice.240
  51.9 1.1 slice.233
  53.8 1.2 slice.227
  55.0 118.5 %all-gather.3.cloned.1.call-done = f32[3,24,32,2048]{3,2,1,0:T(8,128)} async-done(((f32[3,24,32,128]{3,2,1,0:T(8,128)}), f32[3,24,32,2048]{3,2,1,0:T(8,128)}) %all-gather.3.cloned.1.call-update) | async-done | bytes 18874384 | tf_op jit(solution)/shard_map/all_gather | solution.py:91
  173.5 18.5 %fusion.2 = f32[3,24,32,256]{3,2,1,0:T(8,128)S(1)} fusion(f32[3,24,32,2048]{3,2,1,0:T(8,128)} %all-gather.3.cloned.1.call-done, f32[2048,128]{1,0:T(8,128)} %get-tuple-element.50, f32[2048,128]{1,0:T(8,128)} %get-tuple-element.51, f32[32,256]{1,0:T(8,128)S(1)} %pad_maximum_fusion.11), kind=kOutput, calls=%fused_computation.24 | convolution fusion | flops 14496628736 | bytes 23363584 | tf_op jit(solution)/shard_map/dot_general | solution.py:70
  192.0 2.0 fusion.44
  195.7 1.2 fusion.34
  197.5 1.2 fusion.33
  198.7 1.3 fusion.7
  200.0 1.3 fusion.10
  202.7 1.3 fusion.6
  204.0 3.7 collective-permute-start.6
  208.3 3.1 collective-permute-start.5
  212.0 2.4 copy.31
  214.4 2.4 copy.30
  216.8 15.9 %fusion.28 = (f32[24,128,128]{2,1,0:T(8,128)S(1)}, f32[24,128,128]{2,1,0:T(8,128)S(1)}, pred[24,128,128]{2,1,0:T(8,128)(4,1)S(1)}, pred[24,128,128]{2,1,0:T(8,12...) fusion(f32[23,128,128]{2,1,0:T(8,128)} %fusion.34, ...), kind=kLoop, calls=%fused_computation.57 | loop fusion | flops 16121856 | bytes 17289280 | tf_op jit(solution)/shard_map/add | solution.py:153
  233.9 1.0 copy-done.6
  234.9 1.3 copy-done.13
  236.3 14.9 %fusion.25 = (f32[24,128,128]{2,1,0:T(8,128)S(1)}, f32[24,128,128]{2,1,0:T(8,128)}) fusion(f32[24,128,127]{2,1,0:T(8,128)S(1)} %copy-done.13, f32[24,128,1]{2,1,0:T(8,128)S(1)} %copy-done.14, f32[24,128,128]{2,1,0:T(8,128)S(1)} %get-tuple-element.16, f32[23,128,128]{2,1,0:T(8,128)S(1)} %copy-done.26, f32[1,128,128]{2,1,0:T(8,128)} %bitcast.34, ...), kind=kLoop, calls=%fused_computation.52 | loop fusion | flops 13369344 | bytes 14156352 | tf_op jit(solution)/shard_map/add | solution.py:149
  251.3 13.2 %fusion.32 = f32[24,128,128]{2,1,0:T(8,128)S(1)} fusion(f32[24,128,128]{2,1,0:T(8,128)S(1)} %get-tuple-element.7, f32[24,128,127]{2,1,0:T(8,128)S(1)} %copy-done.15, f32[24,128,1]{2,1,0:T(8,128)S(1)} %copy-done.18, f32[24,127,128]{2,1,0:T(8,128)S(1)} %bitcast.87, f32[24,128,128]{2,1,0:T(8,128)S(1)} %copy-done.2, f32[128]{0:T(128)S(1)} %copy-done.42, ...), kind=kLoop, calls=%fused_computation.62 | loop fusion | flops 13369344 | bytes 12572224 | tf_op jit(solution)/shard_map/add | solution.py:156
  264.5 1.2 pad_maximum_fusion.7
  266.0 2.4 slice.257
  268.5 1.1 slice.255
  269.6 127.1 %all-gather.5.cloned.1.call-done = f32[3,24,32,2048]{3,2,1,0:T(8,128)} async-done(((f32[3,24,32,128]{3,2,1,0:T(8,128)}), f32[3,24,32,2048]{3,2,1,0:T(8,128)}) %all-gather.5.cloned.1.call-update) | async-done | bytes 18874384 | tf_op jit(solution)/shard_map/all_gather | solution.py:91
  396.7 18.2 %fusion.3 = f32[3,24,32,256]{3,2,1,0:T(8,128)S(1)} fusion(f32[3,24,32,2048]{3,2,1,0:T(8,128)} %all-gather.5.cloned.1.call-done, f32[2048,128]{1,0:T(8,128)S(1)} %copy-done.8, f32[2048,128]{1,0:T(8,128)S(1)} %copy-done.9, f32[32,256]{1,0:T(8,128)S(1)} %copy-done.30), kind=kOutput, calls=%fused_computation.25 | convolution fusion | flops 14496628736 | bytes 23363584 | tf_op jit(solution)/shard_map/dot_general | solution.py:70
  414.9 2.0 fusion.43
  417.0 1.2 slice-done
  418.2 1.3 pad_maximum_fusion.5
  420.0 1.3 pad_maximum_fusion.4
  421.8 1.3 pad_maximum_fusion.3
  (129 shorter events, 12.7 us)
Async XLA Ops:
  7.2 3.6 copy-start
  7.2 166.3 %all-gather.3.cloned.1.call-start = ((), (), s32[]{:S(2)}) async-start(), calls=%async_computation | async-start | bytes 20054016 | tf_op jit(solution)/shard_map/all_gather | solution.py:91
  7.2 11.5 %copy-start.7 = (f32[24,128,128]{2,1,0:T(8,128)S(1)}, f32[24,128,128]{2,1,0:T(8,128)}, u32[]{:S(2)}) copy-start(f32[24,128,128]{2,1,0:T(8,128)} %param.11) | copy-start | bytes 4718596
  9.3 20.2 %collective-permute-start = (f32[24,128]{1,0:T(8,128)S(1)}, f32[24,128]{1,0:T(8,128)S(1)}, u32[]{:S(2)}, u32[]{:S(2)}) collective-permute-start(f32[24,128]{1,0:T(8,128)S(1)} %bitcast.94), channel_id=1, source_target_pairs={{8,0},{16,8},{24,16},{32,24},{40,32},{48,40},{56,48},{64,56},{72,6... | collective-permute-start | bytes 36872 | tf_op jit(solution)/shard_map/ppermute | solution.py:17
  11.2 16.6 %collective-permute-start.3 = (f32[24,128]{1,0:T(8,128)S(1)}, f32[24,128]{1,0:T(8,128)S(1)}, u32[]{:S(2)}, u32[]{:S(2)}) collective-permute-start(f32[24,128]{1,0:T(8,128)S(1)} %bitcast.96), channel_id=1, source_target_pairs={{8,0},{16,8},{24,16},{32,24},{40,32},{48,40},{56,48},{64,56},{72,6... | collective-permute-start | bytes 36872 | tf_op jit(solution)/shard_map/ppermute | solution.py:17
  17.4 13.7 %collective-permute-start.2 = (f32[128,128]{1,0:T(8,128)S(1)}, f32[128,128]{1,0:T(8,128)S(1)}, u32[]{:S(2)}, u32[]{:S(2)}) collective-permute-start(f32[128,128]{1,0:T(8,128)S(1)} %slice_bitcast_fusion.6), channel_id=1, source_target_pairs={{1,0},{2,1},{3,2},{4,3},{5,4},{6,5},{7,6},{9,8},{10,9},{11,10},{12... | collective-permute-start | bytes 196616 | tf_op jit(solution)/shard_map/ppermute | solution.py:23
  18.7 12.4 %collective-permute-start.1 = (f32[128,128]{1,0:T(8,128)S(1)}, f32[128,128]{1,0:T(8,128)S(1)}, u32[]{:S(2)}, u32[]{:S(2)}) collective-permute-start(f32[128,128]{1,0:T(8,128)S(1)} %slice_bitcast_fusion.7), channel_id=1, source_target_pairs={{1,0},{2,1},{3,2},{4,3},{5,4},{6,5},{7,6},{9,8},{10,9},{11,10},{12... | collective-permute-start | bytes 196616 | tf_op jit(solution)/shard_map/ppermute | solution.py:23
  20.0 11.1 %copy-start.39 = (f32[128]{0:T(128)}, f32[128]{0:T(128)S(1)}, u32[]{:S(2)}) copy-start(f32[128]{0:T(128)S(1)} %broadcast_multiply_fusion.3) | copy-start | bytes 1540
  20.1 16.9 %copy-start.43 = (f32[128]{0:T(128)}, f32[128]{0:T(128)S(1)}, u32[]{:S(2)}) copy-start(f32[128]{0:T(128)S(1)} %get-tuple-element.49) | copy-start | bytes 1540
  20.1 11.1 %copy-start.41 = (f32[128]{0:T(128)}, f32[128]{0:T(128)S(1)}, u32[]{:S(2)}) copy-start(f32[128]{0:T(128)S(1)} %iota_add_fusion.2) | copy-start | bytes 1540
  21.3 2.0 copy-start.1
  31.2 5.9 %copy-start.31 = (f32[24,128,128]{2,1,0:T(8,128)S(1)}, f32[24,128,128]{2,1,0:T(8,128)}, u32[]{:S(2)}) copy-start(f32[24,128,128]{2,1,0:T(8,128)} %param.15) | copy-start | bytes 4718596
  36.8 4.0 copy-start.10
  36.8 4.0 copy-start.12
  36.8 2.5 copy-start.20
  36.8 3.0 copy-start.21
  41.9 2.1 copy-start.37
  41.9 2.8 copy-start.45
  43.1 353.6 %all-gather.5.cloned.1.call-start = ((), (), s32[]{:S(2)}) async-start(), calls=%async_computation.1 | async-start | bytes 20054016 | tf_op jit(solution)/shard_map/all_gather | solution.py:91
  44.8 128.7 %copy-start.29 = (f32[32,256]{1,0:T(8,128)}, f32[32,256]{1,0:T(8,128)S(1)}, u32[]{:S(2)}) copy-start(f32[32,256]{1,0:T(8,128)S(1)} %pad_maximum_fusion.11) | copy-start | bytes 98308
  45.1 146.9 %copy-start.32 = (f32[128,128]{1,0:T(8,128)}, f32[128,128]{1,0:T(8,128)S(1)}, u32[]{:S(2)}) copy-start(f32[128,128]{1,0:T(8,128)S(1)} %get-tuple-element.44) | copy-start | bytes 196612
  45.1 146.9 %copy-start.34 = (f32[128,128]{1,0:T(8,128)}, f32[128,128]{1,0:T(8,128)S(1)}, u32[]{:S(2)}) copy-start(f32[128,128]{1,0:T(8,128)S(1)} %get-tuple-element.45) | copy-start | bytes 196612
  51.9 2.0 copy-start.17
  194.1 8.6 %copy-start.22 = (f32[768,128]{1,0:T(8,128)}, f32[768,128]{1,0:T(8,128)S(1)}, u32[]{:S(2)}) copy-start(f32[768,128]{1,0:T(8,128)S(1)} %get-tuple-element.27) | copy-start | bytes 1179652
  195.7 1.8 copy-start.3
  200.0 1.8 copy-start.5
  204.0 10.4 %collective-permute-start.4 = (f32[24,128]{1,0:T(8,128)S(1)}, f32[24,128]{1,0:T(8,128)}, u32[]{:S(2)}, u32[]{:S(2)}) collective-permute-start(f32[24,128]{1,0:T(8,128)S(1)} %fusion.5), channel_id=1, source_target_pairs={{120,0},{0,8},{8,16},{16,24},{24,32},{32,40},{40,48},{48,56},{56,6... | collective-permute-start | bytes 36872 | tf_op jit(solution)/shard_map/ppermute | solution.py:17
  204.0 7.4 %collective-permute-start.7 = (f32[24,128]{1,0:T(8,128)S(1)}, f32[24,128]{1,0:T(8,128)S(1)}, u32[]{:S(2)}, u32[]{:S(2)}) collective-permute-start(f32[24,128]{1,0:T(8,128)S(1)} %fusion.9), channel_id=1, source_target_pairs={{120,0},{0,8},{8,16},{16,24},{24,32},{32,40},{40,48},{48,56},{56,6... | collective-permute-start | bytes 36872 | tf_op jit(solution)/shard_map/ppermute | solution.py:17
  204.0 12.8 %collective-permute-start.6 = (f32[128,128]{1,0:T(8,128)}, f32[128,128]{1,0:T(8,128)}, u32[]{:S(2)}, u32[]{:S(2)}) collective-permute-start(f32[128,128]{1,0:T(8,128)} %fusion.53), channel_id=1, source_target_pairs={{0,1},{1,2},{2,3},{3,4},{4,5},{5,6},{6,7},{8,9},{9,10},{10,11},{11... | collective-permute-start | bytes 196616 | tf_op jit(solution)/shard_map/ppermute | solution.py:23
  208.3 25.6 %collective-permute-start.5 = (f32[128,128]{1,0:T(8,128)}, f32[128,128]{1,0:T(8,128)}, u32[]{:S(2)}, u32[]{:S(2)}) collective-permute-start(f32[128,128]{1,0:T(8,128)} %fusion.54), channel_id=1, source_target_pairs={{0,1},{1,2},{2,3},{3,4},{4,5},{5,6},{6,7},{8,9},{9,10},{10,11},{11... | collective-permute-start | bytes 196616 | tf_op jit(solution)/shard_map/ppermute | solution.py:23
  216.8 17.1 %copy-start.14 = (f32[24,128,1]{2,1,0:T(8,128)S(1)}, f32[24,128,1]{2,1,0:T(8,128)}, u32[]{:S(2)}) copy-start(f32[24,128,1]{2,1,0:T(8,128)} %copy.30) | copy-start | bytes 36868
  216.8 17.1 %copy-start.26 = (f32[23,128,128]{2,1,0:T(8,128)S(1)}, f32[23,128,128]{2,1,0:T(8,128)}, u32[]{:S(2)}) copy-start(f32[23,128,128]{2,1,0:T(8,128)} %fusion.33) | copy-start | bytes 4521988
  232.7 18.6 %copy-start.4 = (f32[24,128,128]{2,1,0:T(8,128)}, f32[24,128,128]{2,1,0:T(8,128)S(1)}, u32[]{:S(2)}) copy-start(f32[24,128,128]{2,1,0:T(8,128)S(1)} %get-tuple-element.16) | copy-start | bytes 4718596
  232.7 18.5 %copy-start.25 = (f32[24,128,128]{2,1,0:T(8,128)}, f32[24,128,128]{2,1,0:T(8,128)S(1)}, u32[]{:S(2)}) copy-start(f32[24,128,128]{2,1,0:T(8,128)S(1)} %get-tuple-element.7) | copy-start | bytes 4718596
  232.7 2.2 copy-start.6
  232.7 3.4 copy-start.13
  232.8 3.5 copy-start.23
  232.8 3.5 copy-start.44
  236.2 15.0 %copy-start.2 = (f32[24,128,128]{2,1,0:T(8,128)S(1)}, f32[24,128,128]{2,1,0:T(8,128)}, u32[]{:S(2)}) copy-start(f32[24,128,128]{2,1,0:T(8,128)} %param.12) | copy-start | bytes 4718596
  236.2 15.0 %copy-start.15 = (f32[24,128,127]{2,1,0:T(8,128)S(1)}, f32[24,128,127]{2,1,0:T(8,128)}, u32[]{:S(2)}) copy-start(f32[24,128,127]{2,1,0:T(8,128)} %fusion.10) | copy-start | bytes 4681732
  236.2 15.0 %copy-start.18 = (f32[24,128,1]{2,1,0:T(8,128)S(1)}, f32[24,128,1]{2,1,0:T(8,128)}, u32[]{:S(2)}) copy-start(f32[24,128,1]{2,1,0:T(8,128)} %copy.31) | copy-start | bytes 36868
  236.3 15.1 %copy-start.40 = (f32[128]{0:T(128)S(1)}, f32[128]{0:T(128)}, u32[]{:S(2)}) copy-start(f32[128]{0:T(128)} %copy-done.39) | copy-start | bytes 1540
  236.3 15.1 %copy-start.42 = (f32[128]{0:T(128)S(1)}, f32[128]{0:T(128)}, u32[]{:S(2)}) copy-start(f32[128]{0:T(128)} %copy-done.41) | copy-start | bytes 1540
  269.6 127.1 %copy-start.8 = (f32[2048,128]{1,0:T(8,128)S(1)}, f32[2048,128]{1,0:T(8,128)}, u32[]{:S(2)}) copy-start(f32[2048,128]{1,0:T(8,128)} %get-tuple-element.50) | copy-start | bytes 3145732
  269.6 127.1 %copy-start.9 = (f32[2048,128]{1,0:T(8,128)S(1)}, f32[2048,128]{1,0:T(8,128)}, u32[]{:S(2)}) copy-start(f32[2048,128]{1,0:T(8,128)} %get-tuple-element.51) | copy-start | bytes 3145732
  269.6 127.1 %copy-start.30 = (f32[32,256]{1,0:T(8,128)S(1)}, f32[32,256]{1,0:T(8,128)}, u32[]{:S(2)}) copy-start(f32[32,256]{1,0:T(8,128)} %copy-done.29) | copy-start | bytes 98308
  269.6 145.3 %copy-start.33 = (f32[128,128]{1,0:T(8,128)S(1)}, f32[128,128]{1,0:T(8,128)}, u32[]{:S(2)}) copy-start(f32[128,128]{1,0:T(8,128)} %copy-done.32) | copy-start | bytes 196612
  269.6 145.4 %copy-start.35 = (f32[128,128]{1,0:T(8,128)S(1)}, f32[128,128]{1,0:T(8,128)}, u32[]{:S(2)}) copy-start(f32[128,128]{1,0:T(8,128)} %copy-done.34) | copy-start | bytes 196612
  (9 other events, 12.4 us)
Sparse Core Ops, SparseCore 0:
  43.2 130.2 all-gather.2
  266.2 130.4 all-gather.4
where the time goes:
time: 431 us; the launch traced here: 430 us
  waiting for transfers between devices  246 us (57%)
  other arithmetic  71.7 us (17%)
  matrix products  40.8 us (9%)
  local copies, waits for them, and re-layouts  39.9 us (9%)
  starting transfers between devices  17.3 us (4%)
  between operations  14.7 us (3%)
    all_gather x2, waiting for transfers between devices, cycle_filter(): portion = lax.all_gather(stacked, 'phi', axis=3, tiled=True)  246 us
    dot_general x2, matrix products, transform(): jnp.dot(flat, basis, precision=lax.Precision.HIGHEST, preferred_element_t...  36.8 us
    add x1, other arithmetic, local(): keep_factor * electric_azimuth  15.9 us
    add x1, other arithmetic, local(): keep_factor * electric_radial  14.9 us
    unnamed x94, local copies, waits for them, and re-layouts  14.4 us
    add x1, other arithmetic, local(): keep_factor * electric_height  13.2 us
    ppermute x4, starting transfers between devices, shifted_2(): return lax.ppermute(block, axis, route)  9.37 us
  transfers between devices with their start and end apart: 10, of which 2 were waited for; matrix products, arithmetic and copies ran while one was open for 11% of the time, Pallas kernels for 0%

commit v1 on v0

--- a/solution.py
+++ b/solution.py
@@ -88,7 +88,9 @@
     offset = lax.axis_index("phi") * local_width
     weights = mode_weights(mode_cutoff, cycle_size)
     local_basis = cycle_basis(offset, local_width, cycle_size)
-    portion = lax.all_gather(stacked, "phi", axis=3, tiled=True)
+    portion = jnp.concatenate(
+        lax.all_to_all(jnp.stack([stacked] * lax.axis_size("phi")), "phi", 0, 0), axis=3
+    )
     spectrum = transform(portion, cycle_basis(jnp.int32(0), portion.shape[3], cycle_size))
     return synthesize(spectrum * weights[None, None], local_basis)
 

time: 431 us -> 832 us (1.93); the launches traced: 430 us -> 818 us
  waiting for transfers between devices: 246 us -> 548 us
  local copies, waits for them, and re-layouts: 39.9 us -> 103 us
  starting transfers between devices: 17.3 us -> 42 us
  between operations: 14.7 us -> 1.84 us
  other arithmetic: 71.7 us -> 82.8 us
    all_to_all x0 -> x2, waiting for transfers between devices: none -> 548 us  [cycle_filter(): lax.all_to_all(jnp.stack([stacked] * lax.axis_size('phi')), 'phi', 0, 0)]
    all_gather x2 -> x0, waiting for transfers between devices: 246 us -> none  [cycle_filter(): portion = lax.all_gather(stacked, 'phi', axis=3, tiled=True)]
    unnamed x94 -> x133, local copies, waits for them, and re-layouts: 14.4 us -> 39.8 us
    another operation x0 -> x2, local copies, waits for them, and re-layouts: none -> 17.8 us  [cycle_filter(): jnp.stack([stacked] * lax.axis_size('phi'))]
    another operation x5 -> x11, local copies, waits for them, and re-layouts: 0.17 us -> 17 us  [filter_three(): stacked = jnp.stack([first[:, :NF], second[:, :NF], third[:, :NF]])]
    all_to_all x0 -> x2, starting transfers between devices: none -> 15.2 us  [cycle_filter(): lax.all_to_all(jnp.stack([stacked] * lax.axis_size('phi')), 'phi', 0, 0)]
    squeeze x2 -> x8, local copies, waits for them, and re-layouts: 0.01 us -> 10.8 us  [the longest x2 4.36 us: filter_three(): filtered[1]]
where the time goes in v1:
time: 832 us; the launch traced here: 818 us
  waiting for transfers between devices  548 us (66%)
  local copies, waits for them, and re-layouts  103 us (12%)
  other arithmetic  82.8 us (10%)
  starting transfers between devices  42 us (5%)
  matrix products  40.7 us (5%)
    all_to_all x2, waiting for transfers between devices, cycle_filter(): lax.all_to_all(jnp.stack([stacked] * lax.axis_size('phi')), 'phi', 0, 0)  548 us
    unnamed x133, local copies, waits for them, and re-layouts  39.8 us
    dot_general x2, matrix products, transform(): jnp.dot(flat, basis, precision=lax.Precision.HIGHEST, preferred_element_t...  36.7 us
    another operation x2, local copies, waits for them, and re-layouts, cycle_filter(): jnp.stack([stacked] * lax.axis_size('phi'))  17.8 us
    another operation x11, local copies, waits for them, and re-layouts, filter_three(): stacked = jnp.stack([first[:, :NF], second[:, :NF], third[:, :NF]])  17 us
    add x1, other arithmetic, local(): keep_factor * electric_azimuth  16.7 us
  transfers between devices with their start and end apart: 10, of which 2 were waited for; matrix products, arithmetic and copies ran while one was open for 11% of the time, Pallas kernels for 0%

profile of v1, /device:TPU:1, one launch (start us, length us, event | category | flops | bytes accessed | tf_op | source)
XLA Modules:
  0.0 818.1 jit_solution(13652951261053159067)
XLA Ops:
  0.7 2.0 copy.74
  7.0 2.0 copy.73
  9.0 6.3 collective-permute-start.3
  18.2 2.0 copy.77
  21.8 3.0 copy.80
  24.8 3.1 copy.86
  27.9 3.1 copy.91
  31.1 6.9 fusion.15
  43.0 1.8 copy.94
  44.8 3.8 slice_bitcast_fusion.4
  48.6 1.8 copy.92
  50.4 1.9 copy.93
  52.4 8.9 %stack.24 = f32[16,3,24,32,128]{4,3,2,1,0:T(8,128)} broadcast(f32[3,24,32,128]{3,2,1,0:T(8,128)S(1)} %pad_maximum_fusion.6), dimensions={1,2,3,4} | broadcast | bytes 20054016 | tf_op jit(solution)/shard_map/stack | solution.py:92
  61.3 6.3 all-to-all-start
  67.7 3.1 copy.65
  72.5 5.3 fusion.40
  80.2 1.7 slice.240
  83.5 271.1 %all-to-all-done = f32[16,3,24,32,128]{4,3,2,1,0:T(8,128)} async-done(((f32[16,3,24,32,128]{4,3,2,1,0:T(8,128)}), f32[16,3,24,32,128]{4,3,2,1,0:T(8,128)}, u32[]{:S(2)}, u32[]{:S(2)}) %all-to-all-start) | async-done | bytes 18874400 | tf_op jit(solution)/shard_map/all_to_all | solution.py:92
  354.6 18.4 %fusion.6 = f32[3,24,32,256]{3,2,1,0:T(8,128)S(1)} fusion(f32[2048,128]{1,0:T(8,128)S(1)} %get-tuple-element.62, f32[2048,128]{1,0:T(8,128)} %get-tuple-element.63, f32[32,256]{1,0:T(8,128)S(1)} %pad_maximum_fusion.11, f32[16,3,24,32,128]{4,3,2,1,0:T(8,128)} %all-to-all-done), kind=kOutput, calls=%fused_computation.7 | convolution fusion | flops 14496628736 | bytes 23363584 | tf_op jit(solution)/shard_map/dot_general | solution.py:70
  373.0 2.0 fusion.43
  376.7 3.7 slice_maximum_fusion.3
  382.4 1.6 copy.97
  384.0 3.7 slice_maximum_fusion
  390.1 7.2 collective-permute-start.7
  397.3 4.6 collective-permute-start.6
  402.0 4.1 collective-permute-start.5
  407.7 2.5 slice_maximum_fusion.4
  413.0 16.7 %fusion.29 = (f32[24,128,128]{1,0,2:T(8,128)}, f32[24,128,128]{1,0,2:T(8,128)S(1)}, pred[24,128,128]{1,0,2:T(8,128)(4,1)S(1)}, pred[24,128,128]{1,0,2:T(8,128)(4...) fusion(f32[23,128,128]{1,0,2:T(8,128)} %slice_maximum_fusion.1,, ...), kind=kLoop, calls=%fused_computation.42 | loop fusion | flops 16121856 | bytes 17289280 | tf_op jit(solution)/shard_map/add | solution.py:155
  433.6 13.5 %fusion.33 = f32[24,128,128]{1,0,2:T(8,128)S(1)} fusion(f32[24,128,128]{1,0,2:T(8,128)S(1)} %get-tuple-element.19, f32[24,128,127]{1,0,2:T(8,128)S(1)} %copy-done.34, f32[24,128,1]{1,0,2:T(8,128)} %bitcast.43, f32[24,127,128]{1,0,2:T(8,128)S(1)} %bitcast.95, f32[24,128,128]{1,0,2:T(8,128)S(1)} %copy-done.9, f32[128]{0:T(128)S(1)} %copy-done.55, ...), kind=kLoop, calls=%fused_computation.47 | loop fusion | flops 13369344 | bytes 12572224 | tf_op jit(solution)/shard_map/add | solution.py:158
  449.6 2.6 copy.105
  452.2 16.6 %fusion.26 = (f32[24,128,128]{1,0,2:T(8,128)S(1)}, f32[24,128,128]{1,0,2:T(8,128)}) fusion(f32[24,128,127]{1,0,2:T(8,128)S(1)} %slice_maximum_fusion.4, f32[24,128,1]{1,0,2:T(8,128)S(1)} %bitcast.108, f32[24,128,128]{1,0,2:T(8,128)} %copy-done.10, f32[23,128,128]{1,0,2:T(8,128)} %slice_maximum_fusion.2, f32[1,128,128]{1,0,2:T(1,128)} %bitcast.36, ...), kind=kLoop, calls=%fused_computation.37 | loop fusion | flops 13369344 | bytes 14156352 | tf_op jit(solution)/shard_map/add | solution.py:151
  474.0 8.9 %stack.29 = f32[16,3,24,32,128]{4,3,2,1,0:T(8,128)} broadcast(f32[3,24,32,128]{3,2,1,0:T(8,128)S(1)} %pad_maximum_fusion.7), dimensions={1,2,3,4} | broadcast | bytes 20054016 | tf_op jit(solution)/shard_map/stack | solution.py:92
  482.9 8.9 %all-to-all-start.1 = ((f32[16,3,24,32,128]{4,3,2,1,0:T(8,128)}), f32[16,3,24,32,128]{4,3,2,1,0:T(8,128)}, u32[]{:S(2)}, u32[]{:S(2)}) async-start(f32[16,3,24,32,128]{4,3,2,1,0:T(8,128)} %stack.29), calls=%async_computation.1 | async-start | bytes 37748736 | tf_op jit(solution)/shard_map/all_to_all | solution.py:92
  491.8 1.6 slice.266
  493.5 1.7 slice.264
  496.8 1.6 copy.113
  498.4 1.6 copy.114
  500.1 3.2 copy.115
  503.3 276.6 %all-to-all-done.1 = f32[16,3,24,32,128]{4,3,2,1,0:T(8,128)} async-done(((f32[16,3,24,32,128]{4,3,2,1,0:T(8,128)}), f32[16,3,24,32,128]{4,3,2,1,0:T(8,128)}, u32[]{:S(2)}, u32[]{:S(2)}) %all-to-all-start.1) | async-done | bytes 18874400 | tf_op jit(solution)/shard_map/all_to_all | solution.py:92
  779.8 18.3 %fusion.9 = f32[3,24,32,256]{3,2,1,0:T(8,128)S(1)} fusion(f32[2048,128]{1,0:T(8,128)S(1)} %copy-done.28, f32[2048,128]{1,0:T(8,128)S(1)} %copy-done.29, f32[32,256]{1,0:T(8,128)S(1)} %copy-done.44, f32[16,3,24,32,128]{4,3,2,1,0:T(8,128)} %all-to-all-done.1), kind=kOutput, calls=%fused_computation.8 | convolution fusion | flops 14496628736 | bytes 23363584 | tf_op jit(solution)/shard_map/dot_general | solution.py:70
  798.1 2.0 fusion.42
  802.6 1.9 pad_maximum_fusion.2
  804.5 1.7 copy.112
  806.1 2.7 copy.108
  808.9 1.9 pad_maximum_fusion.1
  810.8 1.7 copy.111
  814.0 1.9 pad_maximum_fusion
  815.9 1.7 copy.110
  (181 shorter events, 47.3 us)
Async XLA Ops:
  0.6 3.5 slice-start.3
  0.6 4.9 slice-start.2
  2.7 15.5 %copy-start.8 = (f32[24,128,128]{1,0,2:T(8,128)}, f32[24,128,128]{1,0,2:T(8,128)S(1)}, u32[]{:S(2)}) copy-start(f32[24,128,128]{1,0,2:T(8,128)S(1)} %copy.74) | copy-start | bytes 4718596
  2.7 28.4 %collective-permute-start = (f32[24,128]{1,0:T(8,128)S(1)}, f32[24,128]{1,0:T(8,128)S(1)}, u32[]{:S(2)}, u32[]{:S(2)}) collective-permute-start(f32[24,128]{1,0:T(8,128)S(1)} %slice_bitcast_fusion.7), channel_id=1, source_target_pairs={{8,0},{16,8},{24,16},{32,24},{40,32},{48,40},{56,48},{64,56},{72,6... | collective-permute-start | bytes 36872 | tf_op jit(solution)/shard_map/ppermute | solution.py:17
  4.3 26.8 %collective-permute-start.1 = (f32[128,128]{0,1:T(8,128)S(1)}, f32[128,128]{0,1:T(8,128)S(1)}, u32[]{:S(2)}, u32[]{:S(2)}) collective-permute-start(f32[128,128]{0,1:T(8,128)S(1)} %bitcast.106), channel_id=1, source_target_pairs={{1,0},{2,1},{3,2},{4,3},{5,4},{6,5},{7,6},{9,8},{10,9},{11,10},{12... | collective-permute-start | bytes 196616 | tf_op jit(solution)/shard_map/ppermute | solution.py:23
  5.7 25.4 %collective-permute-start.2 = (f32[128,128]{0,1:T(8,128)S(1)}, f32[128,128]{0,1:T(8,128)S(1)}, u32[]{:S(2)}, u32[]{:S(2)}) collective-permute-start(f32[128,128]{0,1:T(8,128)S(1)} %bitcast.107), channel_id=1, source_target_pairs={{1,0},{2,1},{3,2},{4,3},{5,4},{6,5},{7,6},{9,8},{10,9},{11,10},{12... | collective-permute-start | bytes 196616 | tf_op jit(solution)/shard_map/ppermute | solution.py:23
  8.9 22.1 %copy-start = (f32[24,128,128]{1,0,2:T(8,128)}, f32[24,128,128]{1,0,2:T(8,128)S(1)}, u32[]{:S(2)}) copy-start(f32[24,128,128]{1,0,2:T(8,128)S(1)} %copy.73) | copy-start | bytes 4718596
  9.0 29.5 %collective-permute-start.3 = (f32[24,128]{1,0:T(8,128)S(1)}, f32[24,128]{1,0:T(8,128)S(1)}, u32[]{:S(2)}, u32[]{:S(2)}) collective-permute-start(f32[24,128]{1,0:T(8,128)S(1)} %slice_bitcast_fusion.6), channel_id=1, source_target_pairs={{8,0},{16,8},{24,16},{32,24},{40,32},{48,40},{56,48},{64,56},{72,6... | collective-permute-start | bytes 36872 | tf_op jit(solution)/shard_map/ppermute | solution.py:17
  15.2 15.8 %copy-start.52 = (f32[128]{0:T(128)}, f32[128]{0:T(128)S(1)}, u32[]{:S(2)}) copy-start(f32[128]{0:T(128)S(1)} %broadcast_multiply_fusion.3) | copy-start | bytes 1540
  15.2 23.2 %copy-start.56 = (f32[128]{0:T(128)}, f32[128]{0:T(128)S(1)}, u32[]{:S(2)}) copy-start(f32[128]{0:T(128)S(1)} %get-tuple-element.61) | copy-start | bytes 1540
  15.3 15.8 %copy-start.54 = (f32[128]{0:T(128)}, f32[128]{0:T(128)S(1)}, u32[]{:S(2)}) copy-start(f32[128]{0:T(128)S(1)} %iota_add_fusion.2) | copy-start | bytes 1540
  31.1 7.4 copy-start.30
  61.3 293.3 %all-to-all-start = ((f32[16,3,24,32,128]{4,3,2,1,0:T(8,128)}), f32[16,3,24,32,128]{4,3,2,1,0:T(8,128)}, u32[]{:S(2)}, u32[]{:S(2)}) async-start(f32[16,3,24,32,128]{4,3,2,1,0:T(8,128)} %stack.24), calls=%async_computation | async-start | bytes 37748736 | tf_op jit(solution)/shard_map/all_to_all | solution.py:92
  67.6 3.8 copy-start.51
  67.7 4.4 copy-start.58
  70.7 7.1 copy-start.22
  72.2 282.4 %copy-start.43 = (f32[32,256]{1,0:T(8,128)}, f32[32,256]{1,0:T(8,128)S(1)}, u32[]{:S(2)}) copy-start(f32[32,256]{1,0:T(8,128)S(1)} %pad_maximum_fusion.11) | copy-start | bytes 98308
  72.5 300.5 %copy-start.45 = (f32[128,128]{1,0:T(8,128)}, f32[128,128]{1,0:T(8,128)S(1)}, u32[]{:S(2)}) copy-start(f32[128,128]{1,0:T(8,128)S(1)} %get-tuple-element.56) | copy-start | bytes 196612
  72.5 300.5 %copy-start.47 = (f32[128,128]{1,0:T(8,128)}, f32[128,128]{1,0:T(8,128)S(1)}, u32[]{:S(2)}) copy-start(f32[128,128]{1,0:T(8,128)S(1)} %get-tuple-element.57) | copy-start | bytes 196612
  77.8 276.8 %copy-start.27 = (f32[2048,128]{1,0:T(8,128)}, f32[2048,128]{1,0:T(8,128)S(1)}, u32[]{:S(2)}) copy-start(f32[2048,128]{1,0:T(8,128)S(1)} %get-tuple-element.62) | copy-start | bytes 3145732
  376.7 3.7 copy-start.2
  376.7 3.7 copy-start.4
  384.0 3.7 copy-start.6
  384.0 3.7 copy-start.12
  390.1 39.8 %collective-permute-start.7 = (f32[24,128]{1,0:T(8,128)S(1)}, f32[24,128]{1,0:T(8,128)}, u32[]{:S(2)}, u32[]{:S(2)}) collective-permute-start(f32[24,128]{1,0:T(8,128)S(1)} %fusion.58), channel_id=1, source_target_pairs={{120,0},{0,8},{8,16},{16,24},{24,32},{32,40},{40,48},{48,56},{56,6... | collective-permute-start | bytes 36872 | tf_op jit(solution)/shard_map/ppermute | solution.py:17
  397.3 15.0 %collective-permute-start.6 = (f32[128,128]{0,1:T(8,128)S(1)}, f32[128,128]{0,1:T(8,128)S(1)}, u32[]{:S(2)}, u32[]{:S(2)}) collective-permute-start(f32[128,128]{0,1:T(8,128)S(1)} %bitcast.105), channel_id=1, source_target_pairs={{0,1},{1,2},{2,3},{3,4},{4,5},{5,6},{6,7},{8,9},{9,10},{10,11},{11... | collective-permute-start | bytes 196616 | tf_op jit(solution)/shard_map/ppermute | solution.py:23
  402.0 50.2 %collective-permute-start.5 = (f32[128,128]{0,1:T(8,128)}, f32[128,128]{0,1:T(8,128)}, u32[]{:S(2)}, u32[]{:S(2)}) collective-permute-start(f32[128,128]{0,1:T(8,128)} %bitcast.35), channel_id=1, source_target_pairs={{0,1},{1,2},{2,3},{3,4},{4,5},{5,6},{6,7},{8,9},{9,10},{10,11},{11... | collective-permute-start | bytes 196616 | tf_op jit(solution)/shard_map/ppermute | solution.py:23
  407.7 5.3 copy-start.7
  407.7 5.3 copy-start.13
  407.7 5.3 copy-start.15
  411.8 40.4 %collective-permute-start.4 = (f32[24,128]{1,0:T(8,128)}, f32[24,128]{1,0:T(8,128)S(1)}, u32[]{:S(2)}, u32[]{:S(2)}) collective-permute-start(f32[24,128]{1,0:T(8,128)} %fusion.57), channel_id=1, source_target_pairs={{120,0},{0,8},{8,16},{16,24},{24,32},{32,40},{40,48},{48,56},{56,6... | collective-permute-start | bytes 36872 | tf_op jit(solution)/shard_map/ppermute | solution.py:17
  429.7 17.5 %copy-start.35 = (pred[24,128,128]{1,0,2:T(8,128)(4,1)}, pred[24,128,128]{1,0,2:T(8,128)(4,1)S(1)}, u32[]{:S(2)}) copy-start(pred[24,128,128]{1,0,2:T(8,128)(4,1)S(1)} %get-tuple-element.21) | copy-start | bytes 1179652
  429.7 17.5 %copy-start.36 = (pred[24,128,128]{1,0,2:T(8,128)(4,1)}, pred[24,128,128]{1,0,2:T(8,128)(4,1)S(1)}, u32[]{:S(2)}) copy-start(pred[24,128,128]{1,0,2:T(8,128)(4,1)S(1)} %get-tuple-element.22) | copy-start | bytes 1179652
  429.7 17.5 %copy-start.37 = (pred[24,128,128]{1,0,2:T(8,128)(4,1)}, pred[24,128,128]{1,0,2:T(8,128)(4,1)S(1)}, u32[]{:S(2)}) copy-start(pred[24,128,128]{1,0,2:T(8,128)(4,1)S(1)} %get-tuple-element.23) | copy-start | bytes 1179652
  429.7 17.5 %copy-start.38 = (pred[24,128,128]{1,0,2:T(8,128)(4,1)}, pred[24,128,128]{1,0,2:T(8,128)(4,1)S(1)}, u32[]{:S(2)}) copy-start(pred[24,128,128]{1,0,2:T(8,128)(4,1)S(1)} %get-tuple-element.24) | copy-start | bytes 1179652
  429.7 17.5 %copy-start.39 = (pred[24,128,128]{1,0,2:T(8,128)(4,1)}, pred[24,128,128]{1,0,2:T(8,128)(4,1)S(1)}, u32[]{:S(2)}) copy-start(pred[24,128,128]{1,0,2:T(8,128)(4,1)S(1)} %get-tuple-element.25) | copy-start | bytes 1179652
  429.7 17.5 %copy-start.40 = (pred[24,128,128]{1,0,2:T(8,128)(4,1)}, pred[24,128,128]{1,0,2:T(8,128)(4,1)S(1)}, u32[]{:S(2)}) copy-start(pred[24,128,128]{1,0,2:T(8,128)(4,1)S(1)} %get-tuple-element.26) | copy-start | bytes 1179652
  429.7 17.5 %copy-start.41 = (pred[24,128,128]{1,0,2:T(8,128)(4,1)}, pred[24,128,128]{1,0,2:T(8,128)(4,1)S(1)}, u32[]{:S(2)}) copy-start(pred[24,128,128]{1,0,2:T(8,128)(4,1)S(1)} %get-tuple-element.27) | copy-start | bytes 1179652
  429.7 3.9 copy-start.34
  429.7 3.9 copy-start.53
  429.8 3.9 copy-start.55
  482.9 8.9 %copy-start.26 = (f32[24,128,128]{1,0,2:T(8,128)S(1)}, f32[24,128,128]{1,0,2:T(8,128)}, u32[]{:S(2)}) copy-start(f32[24,128,128]{1,0,2:T(8,128)} %copy-done.25) | copy-start | bytes 4718596
  482.9 296.9 %all-to-all-start.1 = ((f32[16,3,24,32,128]{4,3,2,1,0:T(8,128)}), f32[16,3,24,32,128]{4,3,2,1,0:T(8,128)}, u32[]{:S(2)}, u32[]{:S(2)}) async-start(f32[16,3,24,32,128]{4,3,2,1,0:T(8,128)} %stack.29), calls=%async_computation.1 | async-start | bytes 37748736 | tf_op jit(solution)/shard_map/all_to_all | solution.py:92
  500.1 279.7 %copy-start.28 = (f32[2048,128]{1,0:T(8,128)S(1)}, f32[2048,128]{1,0:T(8,128)}, u32[]{:S(2)}) copy-start(f32[2048,128]{1,0:T(8,128)} %copy-done.27) | copy-start | bytes 3145732
  500.1 279.7 %copy-start.29 = (f32[2048,128]{1,0:T(8,128)S(1)}, f32[2048,128]{1,0:T(8,128)}, u32[]{:S(2)}) copy-start(f32[2048,128]{1,0:T(8,128)} %get-tuple-element.63) | copy-start | bytes 3145732
  500.1 279.7 %copy-start.44 = (f32[32,256]{1,0:T(8,128)S(1)}, f32[32,256]{1,0:T(8,128)}, u32[]{:S(2)}) copy-start(f32[32,256]{1,0:T(8,128)} %copy-done.43) | copy-start | bytes 98308
  503.3 294.9 %copy-start.46 = (f32[128,128]{1,0:T(8,128)S(1)}, f32[128,128]{1,0:T(8,128)}, u32[]{:S(2)}) copy-start(f32[128,128]{1,0:T(8,128)} %copy-done.45) | copy-start | bytes 196612
  503.3 294.9 %copy-start.48 = (f32[128,128]{1,0:T(8,128)S(1)}, f32[128,128]{1,0:T(8,128)}, u32[]{:S(2)}) copy-start(f32[128,128]{1,0:T(8,128)} %copy-done.47) | copy-start | bytes 196612
  (25 other events, 46.5 us)
